TPU v7x, 256 devices: a whole 4x4x8 slice. The times are simulated.
256 devices in a mesh: req: 64 (over z, x, core), tp: 4 (over y).
Axes of the slice: x: 4, y: 4, z: 8, core: 2. Of those that a mesh axis runs over, the one named last changes fastest.
Arguments:
- tokens_new: bfloat16 [64, 16, 2, 1024], P('req'), may hold values from -6 to 6
- prefix_len: int32 [64], replicated, may hold values from 1 to 4096, as said below
- tail_len: int32 [64, 16], P('req'), may hold values from 1 to 512, as said below
- pool_home: int32 [2048], replicated, may hold values from 0 to 63, as said below
- pool_page: int32 [2048], replicated, may hold values from 0 to 31
- slot_page_cache: bfloat16 [2048, 128, 2, 512], P('req', None, None, 'tp'), may hold values from -64 to 64
- tail_cache: bfloat16 [64, 16, 512, 2, 512], P('req', None, None, None, 'tp'), may hold values from -6 to 6
- routes: int32 [64, 16, 2, 8], P('req'), may hold values from 0 to 31, all different within a row; in each aligned block of 32 rows (0 to 31, 32 to 63, ..., all dimensions but the last counted through in order) at most 12 rows name the same one
- norm_gains: float32 [3, 1024], replicated, may hold values from 0.1 to 1.9
- query_weight: bfloat16 [1024, 1024], P(None, 'tp'), may hold values from -0.1875 to 0.1875
- key_value_weight: bfloat16 [1024, 2, 512], P(None, None, 'tp'), may hold values from -0.1875 to 0.1875
- out_weight: bfloat16 [1024, 1024], P('tp'), may hold values from -0.1875 to 0.1875
- router: bfloat16 [1024, 32], replicated, may hold values from -0.375 to 0.375
- expert_in: bfloat16 [64, 1024, 2, 512], P('req', None, None, 'tp'), as said below
- expert_out: bfloat16 [64, 512, 1024], P('req', 'tp'), as said below
- score_weight: float32 [1024], replicated, may hold values from -0.1875 to 0.1875
Outputs:
- layer_out: bfloat16 [64, 16, 2, 1024], P('req')
- row_score: float32 [64, 16, 2], P('req')
Inputs may be any that keep to these rules, and one draw needn't show every extreme that they name: `prefix_len`: some request has exactly 4096 prefix positions. `tail_len`: some sample has exactly 512 tail positions. `pool_home`: entry s * 32 + v describes slot v of the pool of device s of req. Every page 0 to 31 of every request lies in exactly one slot, and one device's pool holds either exactly 1 pages of a request or none of them. `routes`: in the 32 rows of one device no expert is named more than 12 times. `expert_in`: expert table copy c equals copy c mod 32. `expert_out`: expert table copy c equals copy c mod 32.
All inputs are finite; a program needn't handle non-finite values.
Results may differ from a plain program's by a relative error of at most 0.017.
Values may be sent and summed in bfloat16 or wider, within the bound.
A program may use at most 128 MiB of HBM per device.

v0:
```python
import jax
import jax.numpy as jnp
from jax import lax
from jax.sharding import PartitionSpec as P

HEAD_DIM = 64
MOST = 12
EPSILON = 1e-05
ROPE_BASE = 10000.0
LOWEST = -1e30


def rms_scale(values, gain_row):
    widened = values.astype(jnp.float32)
    return (
        widened
        * lax.rsqrt(jnp.mean(widened * widened, axis=-1, keepdims=True) + EPSILON)
        * gain_row
    )


def apply_rotary(vectors, token_positions):
    half_width = vectors.shape[-1] // 2
    frequency = ROPE_BASE ** (-jnp.arange(half_width, dtype=jnp.float32) / half_width)
    angles = token_positions.astype(jnp.float32)[..., None] * frequency
    cosine = jnp.cos(angles)[..., None, :]
    sine_part = jnp.sin(angles)[..., None, :]
    leading = vectors[..., :half_width]
    trailing = vectors[..., half_width:]
    return jnp.concatenate(
        [leading * cosine - trailing * sine_part, trailing * cosine + leading * sine_part], axis=-1
    )


def block_stats(scores, visible):
    block_top = jnp.max(jnp.where(visible, scores, LOWEST), axis=-1)
    weights = jnp.where(
        visible, jnp.exp(jnp.where(visible, scores - block_top[..., None], 0.0)), 0.0
    )
    return (block_top, jnp.sum(weights, axis=-1), weights.astype(jnp.bfloat16))


def shards(
    tokens_new,
    prefix_len,
    tail_len,
    pool_home,
    pool_page,
    slot_page_cache,
    tail_cache,
    routes,
    norm_gains,
    query_weight,
    key_value_weight,
    out_weight,
    router,
    expert_in,
    expert_out,
    score_weight,
):
    device = lax.axis_index("req")
    req_count = lax.axis_size("req")
    samples = tokens_new.shape[1]
    fresh_count = tokens_new.shape[2]
    model_width = tokens_new.shape[3]
    row_count = samples * fresh_count
    head_count = query_weight.shape[1] // HEAD_DIM
    kv_heads = key_value_weight.shape[2] // HEAD_DIM
    query_group_width = head_count // kv_heads
    pool_slots = slot_page_cache.shape[0]
    page_size = slot_page_cache.shape[1]
    slot_cap = max(1, pool_slots // req_count)
    score_scale = HEAD_DIM ** (-0.5)
    flat_tokens = tokens_new.reshape(row_count, model_width)
    normalized_input = rms_scale(flat_tokens, norm_gains[0]).astype(jnp.bfloat16)
    query_vectors = jnp.dot(
        normalized_input, query_weight, preferred_element_type=jnp.float32
    ).reshape(samples, fresh_count, head_count, HEAD_DIM)
    key_value_rows = jnp.dot(
        normalized_input,
        key_value_weight.reshape(model_width, 2 * kv_heads * HEAD_DIM),
        preferred_element_type=jnp.float32,
    ).reshape(samples, fresh_count, 2, kv_heads, HEAD_DIM)
    own_length = jnp.take(prefix_len, device)
    token_positions = (
        own_length + tail_len[0][:, None] + jnp.arange(fresh_count, dtype=jnp.int32)[None, :]
    )
    rotated_query = (
        apply_rotary(query_vectors, token_positions)
        .astype(jnp.bfloat16)
        .reshape(samples, fresh_count, kv_heads, query_group_width, HEAD_DIM)
    )
    key_rot = apply_rotary(key_value_rows[:, :, 0], token_positions).astype(jnp.bfloat16)
    value_new = key_value_rows[:, :, 1].astype(jnp.bfloat16)
    owner_homes = pool_home.reshape(req_count, pool_slots)
    owner_pages = pool_page.reshape(req_count, pool_slots)
    own_home = jnp.take(owner_homes, device, axis=0)
    slot_range = jnp.arange(pool_slots, dtype=jnp.int32)
    cap_range = jnp.arange(slot_cap, dtype=jnp.int32)
    same_home = own_home[:, None] == own_home[None, :]
    earlier = slot_range[:, None] <= slot_range[None, :]
    slot_rank = jnp.sum((same_home & earlier).astype(jnp.int32), axis=0)
    picked_slots = (
        own_home[None, None, :] == jnp.arange(req_count, dtype=jnp.int32)[:, None, None]
    ) & (slot_rank[None, None, :] == cap_range[None, :, None] + 1)
    slot_index = jnp.sum(
        picked_slots.astype(jnp.int32) * slot_range[None, None, :], axis=-1
    ).reshape(-1)
    page_range = jnp.arange(page_size, dtype=jnp.int32)
    outgoing = jnp.take(slot_page_cache, slot_index, axis=0).reshape(
        (req_count, slot_cap) + slot_page_cache.shape[1:]
    )
    arrived = lax.all_to_all(outgoing, "req", split_axis=0, concat_axis=0, tiled=True)
    home_match = owner_homes == device
    home_rank = jnp.cumsum(home_match.astype(jnp.int32), axis=1)
    wanted = home_match[:, None, :] & (home_rank[:, None, :] == cap_range[None, :, None] + 1)
    page_ids = jnp.where(
        jnp.any(wanted, axis=-1),
        jnp.sum(wanted.astype(jnp.int32) * owner_pages[:, None, :], axis=-1),
        -1,
    ).reshape(-1)
    blocks = arrived.reshape(req_count * slot_cap, page_size, 2, kv_heads, HEAD_DIM)
    page_scores = (
        jnp.einsum(
            "sikgd,btkd->bsikgt", rotated_query, blocks[:, :, 0], preferred_element_type=jnp.float32
        )
        * score_scale
    )
    page_spots = page_ids[:, None] * page_size + page_range[None, :]
    page_seen = ((page_spots < own_length) & (page_ids[:, None] >= 0))[:, None, None, None, None, :]
    page_top, page_total, page_weights = block_stats(page_scores, page_seen)
    page_numer = jnp.einsum(
        "bsikgt,btkd->bsikgd", page_weights, blocks[:, :, 1], preferred_element_type=jnp.float32
    )
    tail_count = tail_cache.shape[2]
    tail_block_list = tail_cache[0].reshape(
        samples, tail_count // page_size, page_size, 2, kv_heads, HEAD_DIM
    )
    tail_scores = (
        jnp.einsum(
            "sikgd,sbtkd->sbikgt",
            rotated_query,
            tail_block_list[:, :, :, 0],
            preferred_element_type=jnp.float32,
        )
        * score_scale
    )
    tail_spots = jnp.arange(tail_count, dtype=jnp.int32).reshape(tail_count // page_size, page_size)
    tail_seen = (tail_spots[None] < tail_len[0][:, None, None])[:, :, None, None, None, :]
    tail_top, tail_total, tail_weights = block_stats(tail_scores, tail_seen)
    tail_numer = jnp.einsum(
        "sbikgt,sbtkd->sbikgd",
        tail_weights,
        tail_block_list[:, :, :, 1],
        preferred_element_type=jnp.float32,
    )
    fresh_scores = (
        jnp.einsum("sikgd,sjkd->sikgj", rotated_query, key_rot, preferred_element_type=jnp.float32)
        * score_scale
    )
    fresh_range = jnp.arange(fresh_count, dtype=jnp.int32)
    fresh_seen = (fresh_range[None, :] <= fresh_range[:, None])[None, :, None, None, :]
    fresh_top, fresh_total, fresh_weights = block_stats(fresh_scores, fresh_seen)
    fresh_numer = jnp.einsum(
        "sikgj,sjkd->sikgd", fresh_weights, value_new, preferred_element_type=jnp.float32
    )
    overall = jnp.maximum(
        jnp.maximum(jnp.max(page_top, axis=0), jnp.max(tail_top, axis=1)), fresh_top
    )
    page_factor = jnp.exp(page_top - overall[None])
    tail_factor = jnp.exp(tail_top - overall[:, None])
    fresh_factor = jnp.exp(fresh_top - overall)
    denominator = (
        jnp.sum(page_factor * page_total, axis=0)
        + jnp.sum(tail_factor * tail_total, axis=1)
        + fresh_factor * fresh_total
    )
    numerator = (
        jnp.sum(page_factor[..., None] * page_numer, axis=0)
        + jnp.sum(tail_factor[..., None] * tail_numer, axis=1)
        + fresh_factor[..., None] * fresh_numer
    )
    attn_rows = (
        (numerator / denominator[..., None])
        .astype(jnp.bfloat16)
        .reshape(row_count, head_count * HEAD_DIM)
    )
    attn_part = jnp.dot(attn_rows, out_weight, preferred_element_type=jnp.float32)
    attn_out = lax.psum(attn_part, "tp")
    residual = (flat_tokens.astype(jnp.float32) + attn_out).astype(jnp.bfloat16)
    normed_moe = rms_scale(residual, norm_gains[1]).astype(jnp.bfloat16)
    logits = jnp.dot(normed_moe, router, preferred_element_type=jnp.float32)
    routing = routes.reshape(row_count, -1)
    top_count = routing.shape[1]
    expert_count = router.shape[1]
    expert_range = jnp.arange(expert_count, dtype=jnp.int32)
    route_table = (routing[:, :, None] == expert_range[None, None, :]).astype(jnp.float32)
    picked = jnp.sum(route_table * logits[:, None, :], axis=-1)
    gate_values = jax.nn.softmax(picked, axis=-1)
    local_experts = expert_in.shape[0]
    copies = local_experts * req_count // expert_count
    expert_slot = routing + expert_count * (device % copies)
    onehot = (routing.reshape(-1)[:, None] == expert_range[None, :]).astype(jnp.int32)
    arrival = jnp.sum(jnp.cumsum(onehot, axis=0) * onehot, axis=1) - 1
    target = (expert_slot.reshape(-1) * MOST + arrival).reshape(row_count, top_count)
    buffer = req_count * local_experts * MOST
    hits = (target[None, :, :] == jnp.arange(buffer, dtype=jnp.int32)[:, None, None]).astype(
        jnp.float32
    )
    spread = jnp.sum(hits, axis=-1).astype(jnp.bfloat16)
    combine = jnp.transpose(jnp.sum(hits * gate_values[None], axis=-1))
    outgoing_rows = (
        jnp.dot(spread, normed_moe, preferred_element_type=jnp.float32)
        .astype(jnp.bfloat16)
        .reshape(req_count, local_experts, MOST, model_width)
    )
    gate_up = jnp.einsum(
        "necd,edgf->necgf",
        lax.all_to_all(outgoing_rows, "req", split_axis=0, concat_axis=0, tiled=True),
        expert_in,
        preferred_element_type=jnp.float32,
    )
    hidden = (jax.nn.silu(gate_up[:, :, :, 0]) * gate_up[:, :, :, 1]).astype(jnp.bfloat16)
    result = jnp.einsum("necf,efd->necd", hidden, expert_out, preferred_element_type=jnp.float32)
    returned = lax.all_to_all(
        result.astype(jnp.bfloat16), "req", split_axis=0, concat_axis=0, tiled=True
    ).astype(result.dtype)
    mixed_part = jnp.dot(combine, returned.reshape(buffer, -1), precision=lax.Precision.HIGHEST)
    expert_mix = lax.psum(mixed_part.astype(jnp.bfloat16), "tp").astype(jnp.float32)
    layer_out = (residual.astype(jnp.float32) + expert_mix).astype(jnp.bfloat16)
    final_norm = rms_scale(layer_out, norm_gains[2])
    row_score = jnp.sum(final_norm * score_weight, axis=-1)
    return (
        layer_out.reshape(1, samples, fresh_count, model_width),
        row_score.reshape(1, samples, fresh_count),
    )


def solution(mesh):
    placed = (
        P("req", None, None, None),
        P(),
        P("req", None),
        P(),
        P(),
        P("req", None, None, "tp"),
        P("req", None, None, None, "tp"),
        P("req", None, None, None),
        P(),
        P(None, "tp"),
        P(None, None, "tp"),
        P("tp", None),
        P(),
        P("req", None, None, "tp"),
        P("req", "tp", None),
        P(),
    )
    return jax.shard_map(
        shards,
        mesh=mesh,
        in_specs=placed,
        out_specs=(P("req", None, None, None), P("req", None, None)),
        check_vma=False,
    )
```

profile of v0, /device:TPU:2, one launch (start us, length us, event | category | flops | bytes accessed | tf_op | source)
XLA Modules:
  0.0 399.7 jit_solution(14285597943707223789)
XLA Ops:
  8.8 10.7 %gather_fusion = bf16[64,128,2,128]{3,2,1,0:T(2,128)(2,1)} fusion(bf16[32,128,2,128]{3,2,1,0:T(2,128)(2,1)S(1)} %copy-done, s32[1024]{0:T(1024)S(1)} %pad_clamp_fusion), kind=kCustom, calls=%fused_computation | custom fusion | bytes 8388864 | tf_op jit(solution)/shard_map/jit(_take)/gather | solution.py:110
  19.5 7.9 %fusion.4 = bf16[64,1,128,2,128]{4,3,2,1,0:T(2,128)(2,1)} fusion(bf16[64,128,2,128]{3,2,1,0:T(2,128)(2,1)} %gather_fusion, pred[64]{0:T(512)(128)(4,1)S(1)} %compare_and_fusion), kind=kLoop, calls=%fused_computation.9 | loop fusion | flops 2097152 | bytes 8388672 | tf_op jit(solution)/shard_map/jit(_take)/select_n | solution.py:110
  27.4 12.3 %all-to-all-start = ((bf16[64,1,128,2,128]{4,3,2,1,0:T(2,128)(2,1)}), bf16[64,1,128,2,128]{4,3,2,1,0:T(2,128)(2,1)}, u32[]{:S(2)}, u32[]{:S(2)}) async-start(bf16[64,1,128,2,128]{4,3,2,1,0:T(2,128)(2,1)} %fusion.4), calls=%async_computation | async-start | bytes 8388608 | tf_op jit(solution)/shard_map/all_to_all | solution.py:113
  41.4 11.1 %copy.280 = bf16[1,16,512,2,128]{2,4,3,1,0:T(8,128)(2,1)} copy(bf16[1,16,512,2,128]{4,3,2,1,0:T(2,128)(2,1)} %param.22) | data formatting | bytes 8388608 | tf_op args[6]
  52.6 6.9 %reshape_squeeze.3 = bf16[16,4,128,2,2,64]{2,1,5,4,3,0:T(4,128)(2,1)} reshape(bf16[1,16,512,2,128]{2,4,3,1,0:T(8,128)(2,1)} %copy.280) | data formatting | bytes 8388608 | tf_op jit(solution)/shard_map/reshape;squeeze | solution.py:136
  61.9 5.0 %fusion.85 = (bf16[16,4,128,1,2,64]{2,1,5,4,3,0:T(4,128)(2,1)S(1)}, bf16[16,4,128,1,2,64]{2,1,5,4,3,0:T(4,128)(2,1)}) fusion(bf16[16,4,128,2,2,64]{2,1,5,4,3,0:T(4,128)(2,1)} %reshape_squeeze.3), kind=kLoop, calls=%fused_computation.163 | loop fusion | bytes 8388608 | tf_op jit(solution)/shard_map/slice | solution.py:143
  73.5 62.3 %all-to-all-done = bf16[64,1,128,2,128]{4,3,2,1,0:T(2,128)(2,1)} async-done(((bf16[64,1,128,2,128]{4,3,2,1,0:T(2,128)(2,1)}), bf16[64,1,128,2,128]{4,3,2,1,0:T(2,128)(2,1)}, u32[]{:S(2)}, u32[]{:S(2)}) %all-to-all-start) | async-done | bytes 4194336 | tf_op jit(solution)/shard_map/all_to_all | solution.py:113
  135.8 10.9 %copy.272 = bf16[64,1,128,2,128]{2,4,3,0,1:T(8,128)(2,1)} copy(bf16[64,1,128,2,128]{4,3,2,1,0:T(2,128)(2,1)} %all-to-all-done) | data formatting | bytes 8388608 | tf_op jit(solution)/shard_map/all_to_all | solution.py:113
  146.8 3.1 fusion.6
  149.9 3.3 fusion.7
  154.5 11.1 %copy.345 = bf16[64,1,128,2,128]{2,4,0,3,1:T(8,128)(2,1)} copy(bf16[64,1,128,2,128]{4,3,2,1,0:T(2,128)(2,1)} %all-to-all-done) | data formatting | bytes 8388608 | tf_op jit(solution)/shard_map/reshape | solution.py:122
  165.7 3.0 fusion
  168.7 1.3 fusion.24
  171.4 42.5 %all-reduce.3.cloned.1.call-done = f32[32,1024]{1,0:T(8,128)} async-done(((f32[32,1024]{1,0:T(8,128)}), f32[32,1024]{1,0:T(8,128)}) %all-reduce.3.cloned.1.call-update) | async-done | bytes 131088 | tf_op jit(solution)/shard_map/psum | solution.py:189
  213.9 1.0 fusion.37
  216.3 1.8 convolution_convert_fusion
  218.0 2.4 reshape.522
  220.5 61.7 %all_to_all.15 = bf16[64,1,12,1024]{3,2,1,0:T(8,128)(2,1)S(1)} all-to-all(bf16[64,1,12,1024]{3,2,1,0:T(8,128)(2,1)S(1)} %bitcast.214), channel_id=1, replica_groups=mesh['req'=64,'tp'=4] {'req'}, dimensions={0} | all-to-all | bytes 3145728 | tf_op jit(solution)/shard_map/all_to_all | solution.py:219
  282.2 1.8 fusion.17
  285.5 56.7 %all_to_all.16 = bf16[64,1,12,1024]{3,2,1,0:T(8,128)(2,1)} all-to-all(bf16[64,1,12,1024]{3,2,1,0:T(8,128)(2,1)S(1)} %copy.321), channel_id=1, replica_groups=mesh['req'=64,'tp'=4] {'req'}, dimensions={0} | all-to-all | bytes 3145728 | tf_op jit(solution)/shard_map/all_to_all | solution.py:225
  342.2 3.6 reshape.526
  345.9 2.9 convolution_convert_fusion.2
  348.8 41.5 %all-reduce.5.cloned.1.call-done = bf16[32,1024]{1,0:T(8,128)(2,1)} async-done(((bf16[32,1024]{1,0:T(8,128)(2,1)}), bf16[32,1024]{1,0:T(8,128)(2,1)}) %all-reduce.5.cloned.1.call-update) | async-done | bytes 65552 | tf_op jit(solution)/shard_map/psum | solution.py:229
  390.3 1.0 fusion.33
  (133 shorter events, 18.6 us)
Async XLA Ops:
  7.2 1.6 copy-start
  27.4 12.6 %copy-start.12 = (s32[1,16,2,8]{1,3,2,0:T(8,128)S(1)}, s32[1,16,2,8]{1,3,2,0:T(8,128)}, u32[]{:S(2)}) copy-start(s32[1,16,2,8]{1,3,2,0:T(8,128)} %param.23) | copy-start | bytes 3076
  27.4 12.9 %copy-start.18 = (s32[64]{0:T(128)S(1)}, s32[64]{0:T(128)}, u32[]{:S(2)}) copy-start(s32[64]{0:T(128)} %param.17) | copy-start | bytes 772
  27.4 13.5 %copy-start.4 = (bf16[1024,256]{1,0:T(8,128)(2,1)S(1)}, bf16[1024,256]{1,0:T(8,128)(2,1)}, u32[]{:S(2)}) copy-start(bf16[1024,256]{1,0:T(8,128)(2,1)} %param.25) | copy-start | bytes 1572868
  27.4 13.9 %copy-start.8 = (s32[2048]{0:T(1024)S(1)}, s32[2048]{0:T(1024)}, u32[]{:S(2)}) copy-start(s32[2048]{0:T(1024)} %param.19) | copy-start | bytes 24580
  27.4 14.0 %copy-start.13 = (s32[2048]{0:T(1024)S(1)}, s32[2048]{0:T(1024)}, u32[]{:S(2)}) copy-start(s32[2048]{0:T(1024)} %param.20) | copy-start | bytes 24580
  27.4 108.5 %all-to-all-start = ((bf16[64,1,128,2,128]{4,3,2,1,0:T(2,128)(2,1)}), bf16[64,1,128,2,128]{4,3,2,1,0:T(2,128)(2,1)}, u32[]{:S(2)}, u32[]{:S(2)}) async-start(bf16[64,1,128,2,128]{4,3,2,1,0:T(2,128)(2,1)} %fusion.4), calls=%async_computation | async-start | bytes 8388608 | tf_op jit(solution)/shard_map/all_to_all | solution.py:113
  39.7 174.2 %all-reduce.3.cloned.1.call-start = ((), (), s32[]{:S(2)}) async-start(), calls=%async_computation.3 | async-start | bytes 262144 | tf_op jit(solution)/shard_map/psum | solution.py:189
  52.6 7.0 %copy-start.3 = (bf16[1,16,2,1024]{3,2,1,0:T(2,128)(2,1)S(1)}, bf16[1,16,2,1024]{3,2,1,0:T(2,128)(2,1)}, u32[]{:S(2)}) copy-start(bf16[1,16,2,1024]{3,2,1,0:T(2,128)(2,1)} %param.16) | copy-start | bytes 196612
  52.6 7.8 %copy-start.15 = (s32[1,16]{1,0:T(1,128)S(1)}, s32[1,16]{1,0:T(1,128)}, u32[]{:S(2)}) copy-start(s32[1,16]{1,0:T(1,128)} %param.18) | copy-start | bytes 196
  52.6 7.8 %copy-start.11 = (f32[3,1024]{1,0:T(4,128)S(1)}, f32[3,1024]{1,0:T(4,128)}, u32[]{:S(2)}) copy-start(f32[3,1024]{1,0:T(4,128)} %param.24) | copy-start | bytes 36868
  67.0 2.3 copy-start.5
  149.8 3.3 copy-start.10
  165.7 3.0 copy-start.2
  168.7 1.6 copy-start.6
  168.7 46.3 %copy-start.17 = (bf16[1024,32]{0,1:T(8,128)(2,1)S(1)}, bf16[1024,32]{0,1:T(8,128)(2,1)}, u32[]{:S(2)}) copy-start(bf16[1024,32]{0,1:T(8,128)(2,1)} %param.28) | copy-start | bytes 196612
  171.1 219.2 %all-reduce.5.cloned.1.call-start = ((), (), s32[]{:S(2)}) async-start(), calls=%async_computation.4 | async-start | bytes 131072 | tf_op jit(solution)/shard_map/psum | solution.py:229
  218.0 64.2 %copy-start.16 = (bf16[1,1024,2,128]{3,2,1,0:T(2,128)(2,1)S(1)}, bf16[1,1024,2,128]{3,2,1,0:T(2,128)(2,1)}, u32[]{:S(2)}) copy-start(bf16[1,1024,2,128]{3,2,1,0:T(2,128)(2,1)} %param.29) | copy-start | bytes 1572868
  220.5 63.5 %copy-start.7 = (bf16[1,128,1024]{2,1,0:T(8,128)(2,1)S(1)}, bf16[1,128,1024]{2,1,0:T(8,128)(2,1)}, u32[]{:S(2)}) copy-start(bf16[1,128,1024]{2,1,0:T(8,128)(2,1)} %param.30) | copy-start | bytes 786436
  285.5 107.3 %copy-start.1 = (bf16[32,128,2,128]{3,2,1,0:T(2,128)(2,1)S(1)}, bf16[32,128,2,128]{3,2,1,0:T(2,128)(2,1)}, u32[]{:S(2)}) copy-start(bf16[32,128,2,128]{3,2,1,0:T(2,128)(2,1)} %param.21) | copy-start | bytes 6291460
  342.2 49.7 %copy-start.9 = (f32[1,1024]{1,0:T(1,128)S(1)}, f32[1,1024]{1,0:T(1,128)}, u32[]{:S(2)}) copy-start(f32[1,1024]{1,0:T(1,128)} %get-tuple-element.70) | copy-start | bytes 12292
  342.2 49.7 %copy-start.14 = (f32[1024]{0:T(1024)S(1)}, f32[1024]{0:T(1024)}, u32[]{:S(2)}) copy-start(f32[1024]{0:T(1024)} %param.31) | copy-start | bytes 12292
Sparse Core Ops, SparseCore 0:
  171.2 42.6 all-reduce.2
  348.9 41.2 all-reduce.4
where the time goes:
time: 401 us; the launch traced here: 400 us
  waiting for transfers between devices  146 us (36%)
  blocking collectives  118 us (29%)
  local copies, waits for them, and re-layouts  69.6 us (17%)
  other arithmetic  19.8 us (5%)
  matrix products  17.5 us (4%)
  between operations  15.2 us (4%)
  starting transfers between devices  12.8 us (3%)
    all_to_all x1, waiting for transfers between devices, shards(): lax.all_to_all(outgoing, 'req', split_axis=0, concat_axis=0, tiled=True)  62.3 us
    all_to_all x1, blocking collectives, shards(): lax.all_to_all(outgoing_rows, 'req', split_axis=0, concat_axis=0, tiled=T...  61.7 us
    all_to_all x1, blocking collectives, shards(): lax.all_to_all(result.astype(jnp.bfloat16), 'req', split_axis=0, concat_a...  56.7 us
    psum x1, waiting for transfers between devices, shards(): attn_out = lax.psum(attn_part, 'tp')  42.5 us
    psum x1, waiting for transfers between devices, shards(): lax.psum(mixed_part.astype(jnp.bfloat16), 'tp').astype(jnp.float32)  41.5 us
    unnamed x43, local copies, waits for them, and re-layouts  12.7 us
    all_to_all x1, starting transfers between devices, shards(): lax.all_to_all(outgoing, 'req', split_axis=0, concat_axis=0, tiled=True)  12.3 us
    reshape x1, local copies, waits for them, and re-layouts, shards(): arrived.reshape(req_count * slot_cap, page_size, 2, kv_heads, HEAD_DIM)  11.1 us
  transfers between devices with their start and end apart: 3, of which 3 were waited for; matrix products, arithmetic and copies ran while one was open for 8% of the time, Pallas kernels for 0%

commit v1 on v0

--- a/solution.py
+++ b/solution.py
@@ -186,7 +186,11 @@
         .reshape(row_count, head_count * HEAD_DIM)
     )
     attn_part = jnp.dot(attn_rows, out_weight, preferred_element_type=jnp.float32)
-    attn_out = lax.psum(attn_part, "tp")
+    world_n = lax.axis_size("tp")
+    attn_out = attn_part
+    for i in [k0 for k0 in (1, 2, 4, 8, 16) if k0 < world_n]:
+        oldest = lax.ppermute(attn_out, "tp", tuple(((t, t ^ i) for t in range(world_n))))
+        attn_out = attn_out + oldest
     residual = (flat_tokens.astype(jnp.float32) + attn_out).astype(jnp.bfloat16)
     normed_moe = rms_scale(residual, norm_gains[1]).astype(jnp.bfloat16)
     logits = jnp.dot(normed_moe, router, preferred_element_type=jnp.float32)

time: 401 us -> 365 us (0.910)
  waiting for transfers between devices: 146 us -> 114 us
  starting transfers between devices: 12.8 us -> 17.7 us
    psum x1 -> x0, waiting for transfers between devices: 42.5 us -> none  [shards(): attn_out = lax.psum(attn_part, 'tp')]
    ppermute x0 -> x2, waiting for transfers between devices: none -> 6.54 us  [shards(): lax.ppermute(attn_out, 'tp', tuple(((t, t ^ i) for t in range(world_n))))]
    ppermute x0 -> x2, starting transfers between devices: none -> 5.18 us  [shards(): lax.ppermute(attn_out, 'tp', tuple(((t, t ^ i) for t in range(world_n))))]
    all_to_all x1, blocking collectives: 61.7 us -> 57.3 us  [shards(): lax.all_to_all(outgoing_rows, 'req', split_axis=0, concat_axis=0, tiled=T...]
    unnamed x43 -> x39, local copies, waits for them, and re-layouts: 12.7 us -> 12.7 us
  transfers between devices with their start and end apart: 3 -> 4, of which waited for: 3 -> 4; matrix products, arithmetic and copies ran while one was open for 8% -> 9% of each run, Pallas kernels for 0% -> 0%
where the time goes in v1:
time: 365 us; the launch traced here: 363 us
  waiting for transfers between devices  114 us (31%)
  blocking collectives  114 us (31%)
  local copies, waits for them, and re-layouts  68.4 us (19%)
  starting transfers between devices  17.7 us (5%)
  other arithmetic  17.6 us (5%)
  matrix products  16.9 us (5%)
  between operations  15.2 us (4%)
    all_to_all x1, waiting for transfers between devices, shards(): lax.all_to_all(outgoing, 'req', split_axis=0, concat_axis=0, tiled=True)  64.2 us
    all_to_all x1, blocking collectives, shards(): lax.all_to_all(outgoing_rows, 'req', split_axis=0, concat_axis=0, tiled=T...  57.3 us
    all_to_all x1, blocking collectives, shards(): lax.all_to_all(result.astype(jnp.bfloat16), 'req', split_axis=0, concat_a...  56.7 us
    psum x1, waiting for transfers between devices, shards(): lax.psum(mixed_part.astype(jnp.bfloat16), 'tp').astype(jnp.float32)  43 us
    unnamed x39, local copies, waits for them, and re-layouts  12.7 us
    all_to_all x1, starting transfers between devices, shards(): lax.all_to_all(outgoing, 'req', split_axis=0, concat_axis=0, tiled=True)  12.3 us
    reshape x1, local copies, waits for them, and re-layouts, shards(): arrived.reshape(req_count * slot_cap, page_size, 2, kv_heads, HEAD_DIM)  11.1 us
    all_to_all x1, local copies, waits for them, and re-layouts, shards(): lax.all_to_all(outgoing, 'req', split_axis=0, concat_axis=0, tiled=True)  10.9 us
  transfers between devices with their start and end apart: 4, of which 4 were waited for; matrix products, arithmetic and copies ran while one was open for 9% of the time, Pallas kernels for 0%

profile of v1, /device:TPU:2, one launch (start us, length us, event | category | flops | bytes accessed | tf_op | source)
XLA Modules:
  0.0 363.4 jit_solution(620903256921395651)
XLA Ops:
  8.8 10.7 %gather_fusion = bf16[64,128,2,128]{3,2,1,0:T(2,128)(2,1)} fusion(bf16[32,128,2,128]{3,2,1,0:T(2,128)(2,1)S(1)} %copy-done, s32[1024]{0:T(1024)S(1)} %pad_clamp_fusion), kind=kCustom, calls=%fused_computation | custom fusion | bytes 8388864 | tf_op jit(solution)/shard_map/jit(_take)/gather | solution.py:110
  19.5 7.9 %fusion.4 = bf16[64,1,128,2,128]{4,3,2,1,0:T(2,128)(2,1)} fusion(bf16[64,128,2,128]{3,2,1,0:T(2,128)(2,1)} %gather_fusion, pred[64]{0:T(512)(128)(4,1)S(1)} %compare_and_fusion), kind=kLoop, calls=%fused_computation.9 | loop fusion | flops 2097152 | bytes 8388672 | tf_op jit(solution)/shard_map/jit(_take)/select_n | solution.py:110
  27.4 12.3 %all-to-all-start = ((bf16[64,1,128,2,128]{4,3,2,1,0:T(2,128)(2,1)}), bf16[64,1,128,2,128]{4,3,2,1,0:T(2,128)(2,1)}, u32[]{:S(2)}, u32[]{:S(2)}) async-start(bf16[64,1,128,2,128]{4,3,2,1,0:T(2,128)(2,1)} %fusion.4), calls=%async_computation | async-start | bytes 8388608 | tf_op jit(solution)/shard_map/all_to_all | solution.py:113
  41.4 11.1 %copy.280 = bf16[1,16,512,2,128]{2,4,3,1,0:T(8,128)(2,1)} copy(bf16[1,16,512,2,128]{4,3,2,1,0:T(2,128)(2,1)} %param.22) | data formatting | bytes 8388608 | tf_op args[6]
  52.6 6.9 %reshape_squeeze.3 = bf16[16,4,128,2,2,64]{2,1,5,4,3,0:T(4,128)(2,1)} reshape(bf16[1,16,512,2,128]{2,4,3,1,0:T(8,128)(2,1)} %copy.280) | data formatting | bytes 8388608 | tf_op jit(solution)/shard_map/reshape;squeeze | solution.py:136
  61.4 5.0 %fusion.85 = (bf16[16,4,128,1,2,64]{2,1,5,4,3,0:T(4,128)(2,1)S(1)}, bf16[16,4,128,1,2,64]{2,1,5,4,3,0:T(4,128)(2,1)}) fusion(bf16[16,4,128,2,2,64]{2,1,5,4,3,0:T(4,128)(2,1)} %reshape_squeeze.3), kind=kLoop, calls=%fused_computation.163 | loop fusion | bytes 8388608 | tf_op jit(solution)/shard_map/slice | solution.py:143
  71.7 64.2 %all-to-all-done = bf16[64,1,128,2,128]{4,3,2,1,0:T(2,128)(2,1)} async-done(((bf16[64,1,128,2,128]{4,3,2,1,0:T(2,128)(2,1)}), bf16[64,1,128,2,128]{4,3,2,1,0:T(2,128)(2,1)}, u32[]{:S(2)}, u32[]{:S(2)}) %all-to-all-start) | async-done | bytes 4194336 | tf_op jit(solution)/shard_map/all_to_all | solution.py:113
  135.8 10.9 %copy.272 = bf16[64,1,128,2,128]{2,4,3,0,1:T(8,128)(2,1)} copy(bf16[64,1,128,2,128]{4,3,2,1,0:T(2,128)(2,1)} %all-to-all-done) | data formatting | bytes 8388608 | tf_op jit(solution)/shard_map/all_to_all | solution.py:113
  146.8 3.1 fusion.6
  149.8 3.3 fusion.7
  153.8 11.1 %copy.345 = bf16[64,1,128,2,128]{2,4,0,3,1:T(8,128)(2,1)} copy(bf16[64,1,128,2,128]{4,3,2,1,0:T(2,128)(2,1)} %all-to-all-done) | data formatting | bytes 8388608 | tf_op jit(solution)/shard_map/reshape | solution.py:122
  165.0 3.0 fusion
  169.7 1.6 collective-permute-start
  171.4 3.3 collective-permute-done
  174.8 3.5 collective-permute-start.1
  178.3 3.2 collective-permute-done.1
  183.0 1.8 convolution_convert_fusion
  184.7 2.4 reshape.522
  187.2 57.3 %all_to_all.15 = bf16[64,1,12,1024]{3,2,1,0:T(8,128)(2,1)S(1)} all-to-all(bf16[64,1,12,1024]{3,2,1,0:T(8,128)(2,1)S(1)} %bitcast.214), channel_id=1, replica_groups=mesh['req'=64,'tp'=4] {'req'}, dimensions={0} | all-to-all | bytes 3145728 | tf_op jit(solution)/shard_map/all_to_all | solution.py:223
  244.4 1.8 fusion.17
  247.7 56.7 %all_to_all.16 = bf16[64,1,12,1024]{3,2,1,0:T(8,128)(2,1)} all-to-all(bf16[64,1,12,1024]{3,2,1,0:T(8,128)(2,1)S(1)} %copy.321), channel_id=1, replica_groups=mesh['req'=64,'tp'=4] {'req'}, dimensions={0} | all-to-all | bytes 3145728 | tf_op jit(solution)/shard_map/all_to_all | solution.py:229
  304.5 3.6 reshape.526
  308.1 2.9 convolution_convert_fusion.2
  311.0 43.0 %all-reduce.2.cloned.1.call-done = bf16[32,1024]{1,0:T(8,128)(2,1)} async-done(((bf16[32,1024]{1,0:T(8,128)(2,1)}), bf16[32,1024]{1,0:T(8,128)(2,1)}) %all-reduce.2.cloned.1.call-update) | async-done | bytes 65552 | tf_op jit(solution)/shard_map/psum | solution.py:233
  (131 shorter events, 17.5 us)
Async XLA Ops:
  7.2 1.6 copy-start
  27.4 12.6 %copy-start.10 = (s32[1,16,2,8]{1,3,2,0:T(8,128)S(1)}, s32[1,16,2,8]{1,3,2,0:T(8,128)}, u32[]{:S(2)}) copy-start(s32[1,16,2,8]{1,3,2,0:T(8,128)} %param.23) | copy-start | bytes 3076
  27.4 12.9 %copy-start.16 = (s32[64]{0:T(128)S(1)}, s32[64]{0:T(128)}, u32[]{:S(2)}) copy-start(s32[64]{0:T(128)} %param.17) | copy-start | bytes 772
  27.4 13.5 %copy-start.4 = (bf16[1024,256]{1,0:T(8,128)(2,1)S(1)}, bf16[1024,256]{1,0:T(8,128)(2,1)}, u32[]{:S(2)}) copy-start(bf16[1024,256]{1,0:T(8,128)(2,1)} %param.25) | copy-start | bytes 1572868
  27.4 13.9 %copy-start.8 = (s32[2048]{0:T(1024)S(1)}, s32[2048]{0:T(1024)}, u32[]{:S(2)}) copy-start(s32[2048]{0:T(1024)} %param.19) | copy-start | bytes 24580
  27.4 14.0 %copy-start.11 = (s32[2048]{0:T(1024)S(1)}, s32[2048]{0:T(1024)}, u32[]{:S(2)}) copy-start(s32[2048]{0:T(1024)} %param.20) | copy-start | bytes 24580
  27.4 108.5 %all-to-all-start = ((bf16[64,1,128,2,128]{4,3,2,1,0:T(2,128)(2,1)}), bf16[64,1,128,2,128]{4,3,2,1,0:T(2,128)(2,1)}, u32[]{:S(2)}, u32[]{:S(2)}) async-start(bf16[64,1,128,2,128]{4,3,2,1,0:T(2,128)(2,1)} %fusion.4), calls=%async_computation | async-start | bytes 8388608 | tf_op jit(solution)/shard_map/all_to_all | solution.py:113
  39.7 314.3 %all-reduce.2.cloned.1.call-start = ((), (), s32[]{:S(2)}) async-start(), calls=%async_computation.3 | async-start | bytes 131072 | tf_op jit(solution)/shard_map/psum | solution.py:233
  52.6 7.0 %copy-start.3 = (bf16[1,16,2,1024]{3,2,1,0:T(2,128)(2,1)S(1)}, bf16[1,16,2,1024]{3,2,1,0:T(2,128)(2,1)}, u32[]{:S(2)}) copy-start(bf16[1,16,2,1024]{3,2,1,0:T(2,128)(2,1)} %param.16) | copy-start | bytes 196612
  52.6 7.8 %copy-start.13 = (s32[1,16]{1,0:T(1,128)S(1)}, s32[1,16]{1,0:T(1,128)}, u32[]{:S(2)}) copy-start(s32[1,16]{1,0:T(1,128)} %param.18) | copy-start | bytes 196
  52.6 7.8 %copy-start.9 = (f32[3,1024]{1,0:T(4,128)S(1)}, f32[3,1024]{1,0:T(4,128)}, u32[]{:S(2)}) copy-start(f32[3,1024]{1,0:T(4,128)} %param.24) | copy-start | bytes 36868
  66.4 1.7 copy-start.5
  165.0 3.0 copy-start.2
  168.0 1.6 copy-start.6
  168.0 13.7 %copy-start.15 = (bf16[1024,32]{0,1:T(8,128)(2,1)S(1)}, bf16[1024,32]{0,1:T(8,128)(2,1)}, u32[]{:S(2)}) copy-start(bf16[1024,32]{0,1:T(8,128)(2,1)} %param.28) | copy-start | bytes 196612
  169.7 5.0 %collective-permute-start = (f32[32,1024]{1,0:T(8,128)S(1)}, f32[32,1024]{1,0:T(8,128)S(1)}, u32[]{:S(2)}, u32[]{:S(2)}) collective-permute-start(f32[32,1024]{1,0:T(8,128)S(1)} %fusion.87), channel_id=1, source_target_pairs={{0,1},{1,0},{2,3},{3,2},{4,5},{5,4},{6,7},{7,6},{8,9},{9,8},{10,11... | collective-permute-start | bytes 393224 | tf_op jit(solution)/shard_map/ppermute | solution.py:192
  174.8 6.8 %collective-permute-start.1 = (f32[32,1024]{1,0:T(8,128)S(1)}, f32[32,1024]{1,0:T(8,128)S(1)}, u32[]{:S(2)}, u32[]{:S(2)}) collective-permute-start(f32[32,1024]{1,0:T(8,128)S(1)} %add.198), channel_id=1, source_target_pairs={{0,2},{1,3},{2,0},{3,1},{4,6},{5,7},{6,4},{7,5},{8,10},{9,11},{10,... | collective-permute-start | bytes 393224 | tf_op jit(solution)/shard_map/ppermute | solution.py:192
  184.7 59.7 %copy-start.14 = (bf16[1,1024,2,128]{3,2,1,0:T(2,128)(2,1)S(1)}, bf16[1,1024,2,128]{3,2,1,0:T(2,128)(2,1)}, u32[]{:S(2)}) copy-start(bf16[1,1024,2,128]{3,2,1,0:T(2,128)(2,1)} %param.29) | copy-start | bytes 1572868
  187.2 59.1 %copy-start.7 = (bf16[1,128,1024]{2,1,0:T(8,128)(2,1)S(1)}, bf16[1,128,1024]{2,1,0:T(8,128)(2,1)}, u32[]{:S(2)}) copy-start(bf16[1,128,1024]{2,1,0:T(8,128)(2,1)} %param.30) | copy-start | bytes 786436
  247.7 108.8 %copy-start.1 = (bf16[32,128,2,128]{3,2,1,0:T(2,128)(2,1)S(1)}, bf16[32,128,2,128]{3,2,1,0:T(2,128)(2,1)}, u32[]{:S(2)}) copy-start(bf16[32,128,2,128]{3,2,1,0:T(2,128)(2,1)} %param.21) | copy-start | bytes 6291460
  304.5 51.2 %copy-start.12 = (f32[1024]{0:T(1024)S(1)}, f32[1024]{0:T(1024)}, u32[]{:S(2)}) copy-start(f32[1024]{0:T(1024)} %param.31) | copy-start | bytes 12292
Sparse Core Ops, SparseCore 0:
  311.1 42.7 all-reduce.1
